TPU v7x, 32 devices: a whole 2x2x4 slice. The times are simulated.
32 devices in a mesh: bin: 8 (over z, y), sky: 4 (over x, core).
Axes of the slice: x: 2, y: 2, z: 4, core: 2. Of those that a mesh axis runs over, the one named last changes fastest.
Arguments:
- lensing_maps: bfloat16 [8, 32, 8192], P('bin', 'sky')
- filter_taps: float32 [5, 17], replicated, may hold values from -1.5 to 1.5
- survey_mask: int32 [4, 64], P('sky'), may hold values 0 or 1
- bin_pairs: int32 [36, 2], replicated, may hold values from 0 to 7, as said below
- target_corr: float32 [36, 5, 4], replicated, may hold values from -3 to 3
- pair_weight: float32 [36, 5, 4], replicated, may hold values from 0.3 to 3
Outputs:
- corr_table: float32 [36, 5, 4], replicated
- map_gradient: float32 [8, 32, 8192], P('bin', 'sky')
Inputs may be any that keep to these rules, and one draw needn't show every extreme that they name: `bin_pairs`: every unordered pair of the 8 bins, a bin with itself included, is listed exactly once; the order of the list and of the two bins in a row vary.
All inputs are finite; a program needn't handle non-finite values. No bound on the sum of `survey_mask` on one device may be relied on, other than what follows from the above.
Results may differ from a plain program's by a relative error of at most 0.0015.
Values may be sent and summed in bfloat16 or wider, within the bound.
A program may use at most 64 MiB of HBM per device.

v0:
```python
import jax
import jax.numpy as jnp
from jax import lax
from jax.sharding import PartitionSpec as P

HIGH = lax.Precision.HIGHEST


def with_halo(block, sides, width):
    for axis, dim in sides:
        count = lax.axis_size(axis)
        forward = [(i, i + 1) for i in range(count - 1)]
        backward = [(target, source) for source, target in forward]
        low = lax.ppermute(
            lax.slice_in_dim(block, block.shape[dim] - width, None, axis=dim), axis, forward
        )
        high = lax.ppermute(lax.slice_in_dim(block, 0, width, axis=dim), axis, backward)
        block = jnp.concatenate([low, block, high], axis=dim)
    return block


def shifted(value, axis, steps):
    count = lax.axis_size(axis)
    pairs = [(source, (source + steps) % count) for source in range(count)]
    return lax.ppermute(value, axis, pairs)


def expand_mask(survey_mask):
    values = survey_mask.astype(jnp.float32)
    tiles_x, tiles_y = values.shape
    return jnp.broadcast_to(values[:, None, :, None], (tiles_x, 8, tiles_y, 128)).reshape(
        tiles_x * 8, tiles_y * 128
    )


def smooth(haloed, filter_taps, row_count):
    tap_count = filter_taps.shape[1]
    half_width = (tap_count - 1) // 2
    widened = haloed.astype(jnp.float32)
    across = filter_taps[:, 0, None, None] * widened[None, 0:row_count]
    for a in range(1, tap_count):
        across = across + filter_taps[:, a, None, None] * widened[None, a : a + row_count]
    padded = jnp.pad(across, ((0, 0), (0, 0), (half_width, half_width)))
    col_count = widened.shape[1]
    result = filter_taps[:, 0, None, None] * padded[:, :, 0:col_count]
    for c in range(1, tap_count):
        result = result + filter_taps[:, c, None, None] * padded[:, :, c : c + col_count]
    return result.astype(jnp.bfloat16)


def lagged(left_maps, right_maps, pixmask, lag_count):
    col_count = left_maps.shape[2]
    columns = []
    for offset in range(lag_count):
        joint_mask = pixmask[:, : col_count - offset] * pixmask[:, offset:]
        product = (
            left_maps[:, :, : col_count - offset].astype(jnp.float32)
            * right_maps[:, :, offset:].astype(jnp.float32)
            * joint_mask[None]
        )
        columns.append(jnp.sum(product, axis=(1, 2)))
    return jnp.stack(columns, axis=1)


def adjoint_lags(partner, ahead_w, behind_w, pixmask):
    col_count = partner.shape[2]
    widened = partner.astype(jnp.float32)
    totals = jnp.zeros(partner.shape, jnp.float32)
    for offset in range(ahead_w.shape[1]):
        joint_mask = pixmask[:, : col_count - offset] * pixmask[:, offset:]
        front = jnp.pad(joint_mask[None] * widened[:, :, offset:], ((0, 0), (0, 0), (0, offset)))
        back = jnp.pad(
            joint_mask[None] * widened[:, :, : col_count - offset], ((0, 0), (0, 0), (offset, 0))
        )
        totals = (
            totals + ahead_w[:, offset, None, None] * front + behind_w[:, offset, None, None] * back
        )
    return totals


def adjoint_cols(grads, filter_taps):
    tap_count = filter_taps.shape[1]
    half_width = (tap_count - 1) // 2
    col_count = grads.shape[2]
    padded = jnp.pad(grads, ((0, 0), (0, 0), (half_width, half_width)))
    result = filter_taps[:, tap_count - 1, None, None] * padded[:, :, 0:col_count]
    for c in range(1, tap_count):
        result = (
            result + filter_taps[:, tap_count - 1 - c, None, None] * padded[:, :, c : c + col_count]
        )
    return result


def adjoint_rows(widened, filter_taps, row_count):
    tap_count = filter_taps.shape[1]
    result = filter_taps[:, tap_count - 1, None, None] * widened[:, 0:row_count]
    for a in range(1, tap_count):
        result = (
            result + filter_taps[:, tap_count - 1 - a, None, None] * widened[:, a : a + row_count]
        )
    return jnp.sum(result, axis=0)


def put_block(row_hot, col_hot, values):
    return row_hot[:, None, None, None] * col_hot[None, :, None, None] * values[None, None]


def take_block(table, row_hot, col_hot):
    return jnp.einsum("i,j,ijsl->sl", row_hot, col_hot, table, precision=HIGH)


def per_device(lensing_maps, filter_taps, survey_mask, bin_pairs, target_corr, pair_weight):
    tap_count = filter_taps.shape[1]
    half_width = (tap_count - 1) // 2
    my_strip = lensing_maps[0]
    row_count, col_count = my_strip.shape
    bin_count = lax.axis_size("bin")
    sky_count = lax.axis_size("sky")
    my_bin = lax.axis_index("bin")
    lag_count = pair_weight.shape[2]
    inverse_area = 1.0 / (row_count * sky_count * col_count)
    pixmask = expand_mask(survey_mask)
    haloed = with_halo(my_strip, (("sky", 0),), half_width)
    own_maps = smooth(haloed, filter_taps, row_count)

    def forward_move(carried):
        moved = shifted(carried, "bin", 1)
        return moved

    indices = jnp.arange(bin_count, dtype=jnp.int32)
    mine_hot = (indices == my_bin).astype(jnp.float32)

    def bin_hot(k):
        return (indices == (my_bin - k) % bin_count).astype(jnp.float32)

    visit_count = bin_count - 1
    stored_init = jnp.zeros((visit_count,) + own_maps.shape, own_maps.dtype)

    def keep_visitor(stored, carried, k):
        stored = lax.dynamic_update_index_in_dim(stored, carried, k - 1, 0)
        return stored

    initial = put_block(
        mine_hot, mine_hot, lagged(own_maps, own_maps, pixmask, lag_count) * inverse_area
    )

    def advance(k, state_all):
        carried, tables, stored = state_all
        carried = forward_move(carried)
        stored = keep_visitor(stored, carried, k)
        tables = tables + put_block(
            mine_hot, bin_hot(k), lagged(own_maps, carried, pixmask, lag_count) * inverse_area
        )
        return (carried, tables, stored)

    _, tables, stored = lax.fori_loop(1, bin_count, advance, (own_maps, initial, stored_init))
    pair_table = lax.psum(tables, ("bin", "sky"))
    left_hot = (bin_pairs[:, 0:1] == indices[None, :]).astype(jnp.float32)
    right_hot = (bin_pairs[:, 1:2] == indices[None, :]).astype(jnp.float32)
    corr_table = jnp.einsum("pi,pj,ijsl->psl", left_hot, right_hot, pair_table, precision=HIGH)
    pair_grad = pair_weight * (corr_table - target_corr)
    table_grad = jnp.einsum("pi,pj,psl->ijsl", left_hot, right_hot, pair_grad, precision=HIGH)
    own_block = take_block(table_grad, mine_hot, mine_hot)
    start_grad = adjoint_lags(own_maps, own_block, own_block, pixmask)

    def partner_term(visitor, k):
        other_hot = bin_hot(k)
        return adjoint_lags(
            visitor,
            take_block(table_grad, mine_hot, other_hot),
            take_block(table_grad, other_hot, mine_hot),
            pixmask,
        )

    def reread(k, totals):
        visitor = lax.dynamic_index_in_dim(stored, k - 1, 0, keepdims=False)
        return totals + partner_term(visitor, k)

    totals = lax.fori_loop(1, visit_count + 1, reread, start_grad)
    col_pass = adjoint_cols(totals, filter_taps)
    widened = with_halo(col_pass, (("sky", 1),), half_width)
    map_grad = adjoint_rows(widened, filter_taps, row_count)
    return (corr_table, map_grad[None])


def solution(mesh):
    placed = (P("bin", "sky", None), P(), P("sky", None), P(), P(), P())
    return jax.shard_map(
        per_device,
        mesh=mesh,
        in_specs=placed,
        out_specs=(P(), P("bin", "sky", None)),
        check_vma=False,
    )
```

profile of v0, /device:TPU:9, one launch (start us, length us, event | category | flops | bytes accessed | tf_op | source)
XLA Modules:
  0.0 306.5 jit_solution(4904538330784414321)
XLA Ops:
  0.6 3.7 %collective-permute-start.1 = (bf16[8,8192]{1,0:T(8,128)(2,1)}, bf16[8,8192]{1,0:T(8,128)(2,1)S(1)}, u32[]{:S(2)}, u32[]{:S(2)}) collective-permute-start(bf16[8,8192]{1,0:T(8,128)(2,1)} %bitcast.118), channel_id=1, source_target_pairs={{0,1},{1,2},{2,3},{4,5},{5,6},{6,7},{8,9},{9,10},{10,11},{12,13},{... | collective-permute-start | bytes 393224 | tf_op jit(solution)/shard_map/ppermute | solution.py:14
  14.0 5.9 %fusion.112 = (f32[5,8,8192]{2,1,0:T(8,128)S(1)}, bf16[5,8,8192]{2,1,0:T(8,128)(2,1)S(1)}) fusion(f32[5]{0:T(128)S(1)} %get-tuple-element.778, f32[5]{0:T(128)S(1)} %get-tuple-element.779, f32[5]{0:T(128)S(1)} %get-tuple-element.764, f32[5]{0:T(128)S(1)} %get-tuple-element.765, f32[5]{0:T(128)S(1)} %get-tuple-element.766, f32[5]{0:T(128)S(1)} %get-tuple-element.767, ...), kind=kLoop, calls=%fused_computation.223 | loop fusion | flops 11468800 | bytes 3277140 | tf_op jit(solution)/shard_map/convert_element_type | solution.py:57
  27.2 143.4 %while.42 = (s32[]{:T(128)}, bf16[5,8,8192]{2,1,0:T(8,128)(2,1)}, f32[8,8,5,4]{1,3,2,0:T(4,128)S(1)}, bf16[7,5,8,8192]{3,2,1,0:T(8,128)(2,1)}, s32[]{:T(128)}, /...) while((s32[]{:T(128)}, bf16[5,8,8192]{2,1,0:T(8,128)(2,1)}, ...), condition=%wide.region_9.10_spmd.clone.clone, body=%wide.region_4.9_spmd.clone.clone.sunk | while | flops 6555130 | bytes 10627522 | solution.py:156
  28.6 14.0 %collective-permute-done = bf16[5,8,8192]{2,1,0:T(8,128)(2,1)S(1)} collective-permute-done((bf16[5,8,8192]{2,1,0:T(8,128)(2,1)}, bf16[5,8,8192]{2,1,0:T(8,128)(2,1)S(1)}, u32[]{:S(2)}, u32[]{:S(2)}) %collective-permute-start) | collective-permute-done | bytes 655392 | tf_op jit(solution)/shard_map/while/body/eval_jaxpr/ppermute | solution.py:25
  46.6 16.1 %collective-permute-done = bf16[5,8,8192]{2,1,0:T(8,128)(2,1)S(1)} collective-permute-done((bf16[5,8,8192]{2,1,0:T(8,128)(2,1)}, bf16[5,8,8192]{2,1,0:T(8,128)(2,1)S(1)}, u32[]{:S(2)}, u32[]{:S(2)}) %collective-permute-start) | collective-permute-done | bytes 655392 | tf_op jit(solution)/shard_map/while/body/eval_jaxpr/ppermute | solution.py:25
  66.4 17.7 %collective-permute-done = bf16[5,8,8192]{2,1,0:T(8,128)(2,1)S(1)} collective-permute-done((bf16[5,8,8192]{2,1,0:T(8,128)(2,1)}, bf16[5,8,8192]{2,1,0:T(8,128)(2,1)S(1)}, u32[]{:S(2)}, u32[]{:S(2)}) %collective-permute-start) | collective-permute-done | bytes 655392 | tf_op jit(solution)/shard_map/while/body/eval_jaxpr/ppermute | solution.py:25
  87.8 16.9 %collective-permute-done = bf16[5,8,8192]{2,1,0:T(8,128)(2,1)S(1)} collective-permute-done((bf16[5,8,8192]{2,1,0:T(8,128)(2,1)}, bf16[5,8,8192]{2,1,0:T(8,128)(2,1)S(1)}, u32[]{:S(2)}, u32[]{:S(2)}) %collective-permute-start) | collective-permute-done | bytes 655392 | tf_op jit(solution)/shard_map/while/body/eval_jaxpr/ppermute | solution.py:25
  108.4 18.1 %collective-permute-done = bf16[5,8,8192]{2,1,0:T(8,128)(2,1)S(1)} collective-permute-done((bf16[5,8,8192]{2,1,0:T(8,128)(2,1)}, bf16[5,8,8192]{2,1,0:T(8,128)(2,1)S(1)}, u32[]{:S(2)}, u32[]{:S(2)}) %collective-permute-start) | collective-permute-done | bytes 655392 | tf_op jit(solution)/shard_map/while/body/eval_jaxpr/ppermute | solution.py:25
  130.2 17.0 %collective-permute-done = bf16[5,8,8192]{2,1,0:T(8,128)(2,1)S(1)} collective-permute-done((bf16[5,8,8192]{2,1,0:T(8,128)(2,1)}, bf16[5,8,8192]{2,1,0:T(8,128)(2,1)S(1)}, u32[]{:S(2)}, u32[]{:S(2)}) %collective-permute-start) | collective-permute-done | bytes 655392 | tf_op jit(solution)/shard_map/while/body/eval_jaxpr/ppermute | solution.py:25
  150.9 16.2 %collective-permute-done = bf16[5,8,8192]{2,1,0:T(8,128)(2,1)S(1)} collective-permute-done((bf16[5,8,8192]{2,1,0:T(8,128)(2,1)}, bf16[5,8,8192]{2,1,0:T(8,128)(2,1)S(1)}, u32[]{:S(2)}, u32[]{:S(2)}) %collective-permute-start) | collective-permute-done | bytes 655392 | tf_op jit(solution)/shard_map/while/body/eval_jaxpr/ppermute | solution.py:25
  170.7 47.8 %psum.7 = f32[8,8,5,4]{1,2,0,3:T(8,128)S(1)} all-reduce(f32[8,8,5,4]{1,2,0,3:T(8,128)S(1)} %copy.10), channel_id=1, replica_groups=mesh['bin'=8,'sky'=4] {'bin','sky'}, use_global_device_ids=true, to_apply=%region_10.11 | all-reduce | flops 1280 | bytes 10240 | tf_op jit(solution)/shard_map/psum | solution.py:157
  219.9 4.0 %fusion.78 = f32[5,8,8192]{2,1,0:T(8,128)S(1)} fusion(f32[5,8,8189]{2,1,0:T(8,128)} %get-tuple-element.843, f32[5,8,8189]{2,1,0:T(8,128)} %get-tuple-element.842, f32[5,8,8190]{2,1,0:T(8,128)} %get-tuple-element.841, f32[5,8,8190]{2,1,0:T(8,128)} %get-tuple-element.840, f32[5,8,8191]{2,1,0:T(8,128)} %get-tuple-element.839, ...), kind=kLoop, calls=%fused_computation.126 | loop fusion | flops 4915200 | bytes 9861328 | tf_op jit(solution)/shard_map/add | solution.py:76
  224.0 47.2 %while.43 = (s32[]{:T(128)}, f32[5,8,8192]{2,1,0:T(8,128)S(1)}, s32[]{:T(128)}, f32[8,8,5,4]{1,3,2,0:T(4,128)S(1)}, bf16[7,5,8,8192]{3,2,1,0:T(8,128)(2,1)}, /*i...) while((s32[]{:T(128)}, f32[5,8,8192]{2,1,0:T(8,128)S(1)}, ...), condition=%wide.region_12.13_spmd.clone.clone, body=%wide.region_11.12_spmd.clone.clone.sunk | while | flops 7554175 | bytes 28974256 | solution.py:179
  228.3 2.4 fusion.128
  235.0 2.4 fusion.128
  241.8 2.4 fusion.128
  248.5 2.4 fusion.128
  255.3 2.4 fusion.128
  262.0 2.4 fusion.128
  271.2 5.9 %multiply_add_fusion.3 = f32[5,8,8192]{2,1,0:T(8,128)S(1)} fusion(f32[5,8,8192]{2,1,0:T(8,128)S(1)} %get-tuple-element.629, f32[5]{0:T(128)S(1)} %copy-done.9, f32[5]{0:T(128)S(1)} %copy-done.11, f32[5]{0:T(128)S(1)} %get-tuple-element.764, f32[5]{0:T(128)S(1)} %get-tuple-element.765, f32[5]{0:T(128)S(1)} %get-tuple-element.766, ...), kind=kLoop, calls=%fused_computation.127 | loop fusion | flops 10813440 | bytes 2621780 | tf_op jit(solution)/shard_map/add | solution.py:89
  277.1 5.3 %collective-permute-start.3 = (f32[5,8,8192]{2,1,0:T(8,128)S(1)}, f32[5,8,8192]{2,1,0:T(8,128)S(1)}, u32[]{:S(2)}, u32[]{:S(2)}) collective-permute-start(f32[5,8,8192]{2,1,0:T(8,128)S(1)} %multiply_add_fusion.3), channel_id=1, source_target_pairs={{0,1},{1,2},{2,3},{4,5},{5,6},{6,7},{8,9},{9,10},{10,11},{12,13},{... | collective-permute-start | bytes 3932168 | tf_op jit(solution)/shard_map/ppermute | solution.py:14
  284.9 12.0 %collective-permute-done.3 = f32[5,8,8192]{2,1,0:T(8,128)S(1)} collective-permute-done((f32[5,8,8192]{2,1,0:T(8,128)S(1)}, f32[5,8,8192]{2,1,0:T(8,128)S(1)}, u32[]{:S(2)}, u32[]{:S(2)}) %collective-permute-start.3) | collective-permute-done | bytes 1310752 | tf_op jit(solution)/shard_map/ppermute | solution.py:14
  296.9 4.4 %collective-permute-done.4 = f32[5,8,8192]{2,1,0:T(8,128)S(1)} collective-permute-done((f32[5,8,8192]{2,1,0:T(8,128)S(1)}, f32[5,8,8192]{2,1,0:T(8,128)S(1)}, u32[]{:S(2)}, u32[]{:S(2)}) %collective-permute-start.4) | collective-permute-done | bytes 1310752 | tf_op jit(solution)/shard_map/ppermute | solution.py:17
  301.3 5.2 %fusion.36 = f32[8,8192]{1,0:T(8,128)} fusion(f32[5,8,8192]{2,1,0:T(8,128)S(1)} %multiply_add_fusion.3, f32[5,8,8192]{2,1,0:T(8,128)S(1)} %collective-permute-done.4, f32[5,8,8192]{2,1,0:T(8,128)S(1)} %collective-permute-done.3, f32[5]{0:T(128)S(1)} %copy-done.9, f32[5]{0:T(128)S(1)} %copy-done.11, f32[5]{0:T(128)S(1)} %get-tuple-element.764, ...), kind=kLoop, calls=%fused_computation.75 | loop fusion | flops 15663104 | bytes 4194644 | tf_op jit(solution)/shard_map/reduce_sum | solution.py:101
  (263 shorter events, 80.4 us)
Async XLA Ops:
  0.6 9.4 %collective-permute-start.1 = (bf16[8,8192]{1,0:T(8,128)(2,1)}, bf16[8,8192]{1,0:T(8,128)(2,1)S(1)}, u32[]{:S(2)}, u32[]{:S(2)}) collective-permute-start(bf16[8,8192]{1,0:T(8,128)(2,1)} %bitcast.118), channel_id=1, source_target_pairs={{0,1},{1,2},{2,3},{4,5},{5,6},{6,7},{8,9},{9,10},{10,11},{12,13},{... | collective-permute-start | bytes 393224 | tf_op jit(solution)/shard_map/ppermute | solution.py:14
  4.3 6.5 %collective-permute-start.2 = (bf16[8,8192]{1,0:T(8,128)(2,1)}, bf16[8,8192]{1,0:T(8,128)(2,1)S(1)}, u32[]{:S(2)}, u32[]{:S(2)}) collective-permute-start(bf16[8,8192]{1,0:T(8,128)(2,1)} %bitcast.119), channel_id=1, source_target_pairs={{1,0},{2,1},{3,2},{5,4},{6,5},{7,6},{9,8},{10,9},{11,10},{13,12},{... | collective-permute-start | bytes 393224 | tf_op jit(solution)/shard_map/ppermute | solution.py:17
  9.9 4.0 %copy-start.2 = (f32[5]{0:T(128)}, f32[5]{0:T(128)S(1)}, u32[]{:S(2)}) copy-start(f32[5]{0:T(128)S(1)} %get-tuple-element.775) | copy-start | bytes 64
  9.9 4.0 %copy-start.4 = (f32[5]{0:T(128)}, f32[5]{0:T(128)S(1)}, u32[]{:S(2)}) copy-start(f32[5]{0:T(128)S(1)} %get-tuple-element.776) | copy-start | bytes 64
  10.0 4.0 %copy-start.6 = (f32[5]{0:T(128)}, f32[5]{0:T(128)S(1)}, u32[]{:S(2)}) copy-start(f32[5]{0:T(128)S(1)} %get-tuple-element.777) | copy-start | bytes 64
  10.0 4.0 %copy-start.8 = (f32[5]{0:T(128)}, f32[5]{0:T(128)S(1)}, u32[]{:S(2)}) copy-start(f32[5]{0:T(128)S(1)} %get-tuple-element.778) | copy-start | bytes 64
  10.0 4.0 %copy-start.10 = (f32[5]{0:T(128)}, f32[5]{0:T(128)S(1)}, u32[]{:S(2)}) copy-start(f32[5]{0:T(128)S(1)} %get-tuple-element.779) | copy-start | bytes 64
  27.2 191.7 %copy-start = (f32[36,5,4]{0,2,1:T(4,128)S(1)}, f32[36,5,4]{0,2,1:T(4,128)}, u32[]{:S(2)}) copy-start(f32[36,5,4]{0,2,1:T(4,128)} %param.15) | copy-start | bytes 8644
  27.2 191.7 %copy-start.1 = (f32[36,5,4]{0,2,1:T(4,128)S(1)}, f32[36,5,4]{0,2,1:T(4,128)}, u32[]{:S(2)}) copy-start(f32[36,5,4]{0,2,1:T(4,128)} %param.14) | copy-start | bytes 8644
  27.2 15.4 %collective-permute-start = (bf16[5,8,8192]{2,1,0:T(8,128)(2,1)}, bf16[5,8,8192]{2,1,0:T(8,128)(2,1)S(1)}, u32[]{:S(2)}, u32[]{:S(2)}) collective-permute-start(bf16[5,8,8192]{2,1,0:T(8,128)(2,1)} %get-tuple-element.1039), channel_id=1, source_target_pairs={{0,4},{4,8},{8,12},{12,16},{16,20},{20,24},{24,28},{28,0},{1,5},{5... | collective-permute-start | bytes 1966088 | tf_op jit(solution)/shard_map/while/body/eval_jaxpr/ppermute | solution.py:25
  46.2 16.5 %collective-permute-start = (bf16[5,8,8192]{2,1,0:T(8,128)(2,1)}, bf16[5,8,8192]{2,1,0:T(8,128)(2,1)S(1)}, u32[]{:S(2)}, u32[]{:S(2)}) collective-permute-start(bf16[5,8,8192]{2,1,0:T(8,128)(2,1)} %get-tuple-element.1039), channel_id=1, source_target_pairs={{0,4},{4,8},{8,12},{12,16},{16,20},{20,24},{24,28},{28,0},{1,5},{5... | collective-permute-start | bytes 1966088 | tf_op jit(solution)/shard_map/while/body/eval_jaxpr/ppermute | solution.py:25
  66.3 17.8 %collective-permute-start = (bf16[5,8,8192]{2,1,0:T(8,128)(2,1)}, bf16[5,8,8192]{2,1,0:T(8,128)(2,1)S(1)}, u32[]{:S(2)}, u32[]{:S(2)}) collective-permute-start(bf16[5,8,8192]{2,1,0:T(8,128)(2,1)} %get-tuple-element.1039), channel_id=1, source_target_pairs={{0,4},{4,8},{8,12},{12,16},{16,20},{20,24},{24,28},{28,0},{1,5},{5... | collective-permute-start | bytes 1966088 | tf_op jit(solution)/shard_map/while/body/eval_jaxpr/ppermute | solution.py:25
  87.7 17.0 %collective-permute-start = (bf16[5,8,8192]{2,1,0:T(8,128)(2,1)}, bf16[5,8,8192]{2,1,0:T(8,128)(2,1)S(1)}, u32[]{:S(2)}, u32[]{:S(2)}) collective-permute-start(bf16[5,8,8192]{2,1,0:T(8,128)(2,1)} %get-tuple-element.1039), channel_id=1, source_target_pairs={{0,4},{4,8},{8,12},{12,16},{16,20},{20,24},{24,28},{28,0},{1,5},{5... | collective-permute-start | bytes 1966088 | tf_op jit(solution)/shard_map/while/body/eval_jaxpr/ppermute | solution.py:25
  108.3 18.2 %collective-permute-start = (bf16[5,8,8192]{2,1,0:T(8,128)(2,1)}, bf16[5,8,8192]{2,1,0:T(8,128)(2,1)S(1)}, u32[]{:S(2)}, u32[]{:S(2)}) collective-permute-start(bf16[5,8,8192]{2,1,0:T(8,128)(2,1)} %get-tuple-element.1039), channel_id=1, source_target_pairs={{0,4},{4,8},{8,12},{12,16},{16,20},{20,24},{24,28},{28,0},{1,5},{5... | collective-permute-start | bytes 1966088 | tf_op jit(solution)/shard_map/while/body/eval_jaxpr/ppermute | solution.py:25
  130.1 17.1 %collective-permute-start = (bf16[5,8,8192]{2,1,0:T(8,128)(2,1)}, bf16[5,8,8192]{2,1,0:T(8,128)(2,1)S(1)}, u32[]{:S(2)}, u32[]{:S(2)}) collective-permute-start(bf16[5,8,8192]{2,1,0:T(8,128)(2,1)} %get-tuple-element.1039), channel_id=1, source_target_pairs={{0,4},{4,8},{8,12},{12,16},{16,20},{20,24},{24,28},{28,0},{1,5},{5... | collective-permute-start | bytes 1966088 | tf_op jit(solution)/shard_map/while/body/eval_jaxpr/ppermute | solution.py:25
  150.8 16.2 %collective-permute-start = (bf16[5,8,8192]{2,1,0:T(8,128)(2,1)}, bf16[5,8,8192]{2,1,0:T(8,128)(2,1)S(1)}, u32[]{:S(2)}, u32[]{:S(2)}) collective-permute-start(bf16[5,8,8192]{2,1,0:T(8,128)(2,1)} %get-tuple-element.1039), channel_id=1, source_target_pairs={{0,4},{4,8},{8,12},{12,16},{16,20},{20,24},{24,28},{28,0},{1,5},{5... | collective-permute-start | bytes 1966088 | tf_op jit(solution)/shard_map/while/body/eval_jaxpr/ppermute | solution.py:25
  223.9 47.2 %copy-start.3 = (f32[5]{0:T(128)S(1)}, f32[5]{0:T(128)}, u32[]{:S(2)}) copy-start(f32[5]{0:T(128)} %copy-done.2) | copy-start | bytes 64
  223.9 47.2 %copy-start.5 = (f32[5]{0:T(128)S(1)}, f32[5]{0:T(128)}, u32[]{:S(2)}) copy-start(f32[5]{0:T(128)} %copy-done.4) | copy-start | bytes 64
  223.9 47.2 %copy-start.7 = (f32[5]{0:T(128)S(1)}, f32[5]{0:T(128)}, u32[]{:S(2)}) copy-start(f32[5]{0:T(128)} %copy-done.6) | copy-start | bytes 64
  223.9 47.2 %copy-start.9 = (f32[5]{0:T(128)S(1)}, f32[5]{0:T(128)}, u32[]{:S(2)}) copy-start(f32[5]{0:T(128)} %copy-done.8) | copy-start | bytes 64
  224.0 47.2 %copy-start.11 = (f32[5]{0:T(128)S(1)}, f32[5]{0:T(128)}, u32[]{:S(2)}) copy-start(f32[5]{0:T(128)} %copy-done.10) | copy-start | bytes 64
  277.1 19.8 %collective-permute-start.3 = (f32[5,8,8192]{2,1,0:T(8,128)S(1)}, f32[5,8,8192]{2,1,0:T(8,128)S(1)}, u32[]{:S(2)}, u32[]{:S(2)}) collective-permute-start(f32[5,8,8192]{2,1,0:T(8,128)S(1)} %multiply_add_fusion.3), channel_id=1, source_target_pairs={{0,1},{1,2},{2,3},{4,5},{5,6},{6,7},{8,9},{9,10},{10,11},{12,13},{... | collective-permute-start | bytes 3932168 | tf_op jit(solution)/shard_map/ppermute | solution.py:14
  282.4 18.9 %collective-permute-start.4 = (f32[5,8,8192]{2,1,0:T(8,128)S(1)}, f32[5,8,8192]{2,1,0:T(8,128)S(1)}, u32[]{:S(2)}, u32[]{:S(2)}) collective-permute-start(f32[5,8,8192]{2,1,0:T(8,128)S(1)} %multiply_add_fusion.3), channel_id=1, source_target_pairs={{1,0},{2,1},{3,2},{5,4},{6,5},{7,6},{9,8},{10,9},{11,10},{13,12},{... | collective-permute-start | bytes 3932168 | tf_op jit(solution)/shard_map/ppermute | solution.py:17
where the time goes:
time: 307 us; the launch traced here: 306 us
  waiting for transfers between devices  133 us (43%)
  other arithmetic  79.3 us (26%)
  blocking collectives  47.8 us (16%)
  local copies, waits for them, and re-layouts  22 us (7%)
  starting transfers between devices  14.4 us (5%)
  matrix products  8.21 us (3%)
    ppermute x7, waiting for transfers between devices, shifted(): return lax.ppermute(value, axis, pairs)  116 us
    psum x1, blocking collectives, per_device(): pair_table = lax.psum(tables, ('bin', 'sky'))  47.8 us
    add x7, other arithmetic, reread(): return totals + partner_term(visitor, k)  16.7 us
    mul x24, other arithmetic, adjoint_lags(): joint_mask[None] * widened[:, :, offset:]  14.7 us
    ppermute x2, waiting for transfers between devices, with_halo(): lax.ppermute(lax.slice_in_dim(block, block.shape[dim] - width, None, axis...  12 us
    reduce_sum x29, other arithmetic, lagged(): columns.append(jnp.sum(product, axis=(1, 2)))  11.9 us
    while x42, local copies, waits for them, and re-layouts  8.95 us
    ppermute x2, starting transfers between devices, with_halo(): lax.ppermute(lax.slice_in_dim(block, block.shape[dim] - width, None, axis...  8.95 us
  transfers between devices with their start and end apart: 11, of which 10 were waited for; matrix products, arithmetic and copies ran while one was open for 2% of the time, Pallas kernels for 0%

commit v1 on v0

v1 whole, which is shorter than its diff:
```python
import functools

import jax
import jax.numpy as jnp
from jax import lax
from jax.experimental import pallas as pl
from jax.experimental.pallas import tpu as pltpu
from jax.sharding import PartitionSpec as P

F32 = jnp.float32
BF16 = jnp.bfloat16
XB = 32
MESH = pl.DeviceIdType.MESH
VMEM_LIMIT = 60 * 1024 * 1024


def round_up(n, m):
    return -(-n // m) * m


def halves(value):
    hi = value.astype(BF16)
    lo = (value - hi.astype(F32)).astype(BF16)
    return hi, lo


def mm(a, b):
    return jnp.dot(a, b, preferred_element_type=F32)


def mm3(a, b):
    return mm(a[0], b[0]) + mm(a[0], b[1]) + mm(a[1], b[0])


def place(bins, sky):
    return lax.axis_index("bin") * sky + lax.axis_index("sky")


def greet(me, bins, sky):
    count = bins * sky
    barrier = pltpu.get_barrier_semaphore()

    def hello(k, carry):
        other = lax.rem(me + k, count)
        pl.semaphore_signal(
            barrier, inc=1, device_id=(other // sky, lax.rem(other, sky)), device_id_type=MESH
        )
        return carry

    lax.fori_loop(1, count, hello, 0)
    pl.semaphore_wait(barrier, count - 1)


def band(row, height, width, shift, out_width):
    full = pltpu.roll(
        jnp.broadcast_to(row, (height, width)), width - shift, 1, stride=1, stride_axis=0
    )
    return full[:, :out_width]


def same_row(count):
    left = lax.rem(lax.broadcasted_iota(jnp.int32, (count, count), 0), XB)
    right = lax.rem(lax.broadcasted_iota(jnp.int32, (count, count), 1), XB)
    return (left == right).astype(F32)


def step_kernel(
    bins, sky, scales, lags, groups, chunk, halo, tiles, half, area, src_of, dst_of,
    x_ref, mark_ref, tap_ref, pair_ref, fit_ref,
    result_ref, corr_ref,
    y_ref, marks_ref, hi_ref, lo_ref, g_ref, sums_ref, grad_ref,
    col_ref, adj_ref, part_ref, sky_ref, bin_in_ref, bin_ref,
    send_x, recv_x, send_m, recv_m, send_s, recv_s, send_b, recv_b, send_g, recv_g, own_sem,
):
    count = bins * sky
    strip_rows, width = y_ref.shape[1], y_ref.shape[2]
    out_width = grad_ref.shape[2]
    size = bins * XB
    rows = groups * XB
    my_bin, my_sky = lax.axis_index("bin"), lax.axis_index("sky")
    me = place(bins, sky)
    greet(me, bins, sky)

    def window_copy(other, slot):
        return pltpu.make_async_remote_copy(
            src_ref=src_of(x_ref, other),
            dst_ref=y_ref.at[slot],
            send_sem=send_x.at[other],
            recv_sem=recv_x.at[slot],
            device_id=(other // sky, lax.rem(other, sky)),
            device_id_type=MESH,
        )

    def along(axis, src, dst, send, recv, other, slot):
        return pltpu.make_async_remote_copy(
            src_ref=src,
            dst_ref=dst.at[slot],
            send_sem=send.at[other],
            recv_sem=recv.at[slot],
            device_id=(my_bin, other) if axis == "sky" else (other, my_sky),
            device_id_type=MESH,
        )

    def each(n, mine, act):
        def body(k, carry):
            act(lax.rem(mine + k, n))
            return carry

        lax.fori_loop(1, n, body, 0)

    each(sky, my_sky, lambda o: along("sky", mark_ref, marks_ref, send_m, recv_m, o, my_sky).start())
    each(count, me, lambda o: window_copy(o, me).start())
    own_mark = pltpu.make_async_copy(mark_ref, marks_ref.at[my_sky], own_sem.at[0])
    own_mark.start()
    own = pltpu.make_async_copy(src_of(x_ref, me), y_ref.at[me], own_sem.at[1])
    own.start()

    tall = tap_ref.shape[3]
    row_hi, row_lo, back_hi, back_lo = [], [], [], []
    narrow = round_up(rows + 2 * half + 1, 128)
    for s in range(scales):
        taps, turned = tap_ref[0, s], tap_ref[1, s]
        for at, part in enumerate(halves(band(turned[:, :width], width, width, half, width))):
            col_ref[at, s] = part
        for at, part in enumerate(
            halves(band(taps[:, :width], width, width, half + halo, out_width))
        ):
            adj_ref[at, s] = part
        a, b = halves(band(taps[:, :narrow], rows, narrow, half, rows))
        row_hi.append(a)
        row_lo.append(b)
        back = band(turned[:, :narrow], rows, narrow, half, rows)
        back_hi.append(back)
    row_hi = jnp.concatenate(row_hi, axis=0)
    row_lo = jnp.concatenate(row_lo, axis=0)
    back = halves(jnp.concatenate(back_hi, axis=1))
    diag = same_row(size)
    lanes = lax.broadcasted_iota(jnp.int32, (size, width), 1)
    owned = (lanes >= halo) & (lanes < halo + chunk)
    spot = lax.rem(lax.broadcasted_iota(jnp.int32, (bins, size), 1), XB)
    bin_row = lax.broadcasted_iota(jnp.int32, (bins, size), 0)

    pairs = fit_ref.shape[1]
    first = jnp.broadcast_to(pair_ref[:, 0:1], (pairs, size))
    second = jnp.broadcast_to(pair_ref[:, 1:2], (pairs, size))
    right_hot = lax.broadcasted_iota(jnp.int32, (pairs, size), 1) // XB == second
    weight = jnp.zeros((bins, size), F32)
    target = jnp.zeros((bins, size), F32)
    for i in range(bins):
        hot = right_hot & (first == i)
        weight_row = jnp.sum(jnp.where(hot, fit_ref[0], 0.0), axis=0, keepdims=True)
        target_row = jnp.sum(jnp.where(hot, fit_ref[1], 0.0), axis=0, keepdims=True)
        weight = jnp.where(bin_row == i, weight_row, weight)
        target = jnp.where(bin_row == i, target_row, target)
    sums_ref[...] = jnp.zeros_like(sums_ref)

    each(sky, my_sky, lambda o: along("sky", mark_ref, marks_ref, send_m, recv_m, o, o).wait())
    own_mark.wait()
    each(count, me, lambda o: window_copy(o, o).wait())
    own.wait()

    mark_width = mark_ref.shape[1]
    start = me * chunk - halo + 128
    marks = marks_ref[...].reshape(rows, mark_width)
    marks = pltpu.roll(marks, lax.rem(mark_width - start // 128, mark_width), 1)
    which = (lax.broadcasted_iota(jnp.int32, (rows, width), 1) + start) // 128 - start // 128
    mask = jnp.zeros((rows, width), F32)
    for t in range(tiles):
        mask = jnp.where(which == t, jnp.broadcast_to(marks[:, t : t + 1], (rows, width)), mask)
    masks = [
        jnp.concatenate([mask[g * XB : (g + 1) * XB]] * bins, axis=0) > 0 for g in range(groups)
    ]

    for b in range(bins):
        y = jnp.concatenate([y_ref[b * sky + k].astype(F32) for k in range(sky)], axis=0)
        y = y.astype(BF16)
        hi, lo = halves(mm(row_hi, y) + mm(row_lo, y))
        for s in range(scales):
            for g in range(groups):
                part = slice(s * rows + g * XB, s * rows + (g + 1) * XB)
                hi_ref[g, s, b * XB : (b + 1) * XB, :] = hi[part]
                lo_ref[g, s, b * XB : (b + 1) * XB, :] = lo[part]

    for g in range(groups):

        def forward(s, carry):
            matrix = (col_ref[0, s], col_ref[1, s])
            filtered = mm3((hi_ref[g, s], lo_ref[g, s]), matrix).astype(BF16).astype(F32)
            kept = jnp.where(masks[g], filtered, 0.0)
            g_ref[g, s] = kept.astype(BF16)
            left = jnp.where(owned, kept, 0.0).astype(BF16)
            for l in range(lags):
                right = kept if l == 0 else pltpu.roll(kept, width - l, 1)
                gram = lax.dot_general(
                    left, right.astype(BF16), (((1,), (1,)), ((), ())), preferred_element_type=F32
                )
                gram = jnp.sum((gram * diag).reshape(bins, XB, size), axis=1)
                sums_ref[s * lags + l] = sums_ref[s * lags + l] + gram
            return carry

        lax.fori_loop(0, scales, forward, 0)

    table = jnp.zeros((bins, size), F32)
    for at in range(scales * lags):
        value = sums_ref[at]
        for step in (16, 8, 4, 2, 1):
            value = value + pltpu.roll(value, size - step, 1)
        if at:
            value = pltpu.roll(value, at, 1)
        table = jnp.where(spot == at, value, table)

    part_ref[...] = table
    each(sky, my_sky, lambda o: along("sky", part_ref, sky_ref, send_s, recv_s, o, my_sky).start())
    sky_ref[pl.ds(my_sky, 1)] = table[None]
    each(sky, my_sky, lambda o: along("sky", part_ref, sky_ref, send_s, recv_s, o, o).wait())
    table = sky_ref[0]
    for k in range(1, sky):
        table = table + sky_ref[k]
    bin_in_ref[...] = table
    each(bins, my_bin, lambda o: along("bin", bin_in_ref, bin_ref, send_b, recv_b, o, my_bin).start())
    bin_ref[pl.ds(my_bin, 1)] = table[None]
    each(bins, my_bin, lambda o: along("bin", bin_in_ref, bin_ref, send_b, recv_b, o, o).wait())
    table = bin_ref[0]
    for k in range(1, bins):
        table = table + bin_ref[k]
    table = table * area

    picked = jnp.zeros((pairs, size), F32)
    for i in range(bins):
        picked = jnp.where(first == i, jnp.broadcast_to(table[i : i + 1], (pairs, size)), picked)
    picked = jnp.where(right_hot, picked, 0.0)
    step = size // 2
    while step >= XB:
        picked = picked + pltpu.roll(picked, step, 1)
        step //= 2
    corr_ref[...] = picked

    ahead = jnp.where(spot < scales * lags, weight * (table - target), 0.0)
    spread = jnp.broadcast_to(ahead[:, None, :], (bins, XB, size)).reshape(size, size)
    behind = jnp.sum(jnp.transpose(spread * diag).reshape(bins, XB, size), axis=1)

    def coefficient(values, at):
        value = jnp.where(spot == at, values, 0.0)
        value = pltpu.roll(value, lax.rem(size - at, size), 1)
        for step in (1, 2, 4, 8, 16):
            value = value + pltpu.roll(value, step, 1)
        return value

    for g in range(groups):

        def backward(s, carry):
            maps = g_ref[g, s].astype(F32)
            total_grad = jnp.zeros((size, width), F32)
            for shift in range(1 - lags, lags):
                moved = maps if shift == 0 else pltpu.roll(maps, (width - shift) % width, 1)
                moved = moved.astype(BF16)
                if shift == 0:
                    coef = coefficient(ahead + behind, s * lags)
                elif shift > 0:
                    coef = coefficient(ahead, s * lags + shift)
                else:
                    coef = coefficient(behind, s * lags - shift)
                full = jnp.broadcast_to(coef[:, None, :], (bins, XB, size)).reshape(size, size)
                hi, lo = halves(full * diag)
                total_grad = total_grad + mm(hi, moved) + mm(lo, moved)
            total_grad = jnp.where(masks[g], total_grad, 0.0)
            hi, lo = halves(mm3(halves(total_grad), (adj_ref[0, s], adj_ref[1, s])))
            hi_ref[g, s, :, :out_width] = hi
            lo_ref[g, s, :, :out_width] = lo
            return carry

        lax.fori_loop(0, scales, backward, 0)

    for b in range(bins):
        spots = [(g, s) for s in range(scales) for g in range(groups)]
        rows_of = slice(b * XB, (b + 1) * XB)
        hi = jnp.concatenate([hi_ref[g, s, rows_of, :out_width] for g, s in spots], axis=0)
        lo = jnp.concatenate([lo_ref[g, s, rows_of, :out_width] for g, s in spots], axis=0)
        total_rows = mm3(back, (hi, lo))
        for k in range(sky):
            grad_ref[b * sky + k] = total_rows[k * strip_rows : (k + 1) * strip_rows]

    def grad_copy(other, slot):
        return pltpu.make_async_remote_copy(
            src_ref=grad_ref.at[other],
            dst_ref=dst_of(result_ref, slot),
            send_sem=send_g.at[other],
            recv_sem=recv_g.at[slot],
            device_id=(other // sky, lax.rem(other, sky)),
            device_id_type=MESH,
        )

    each(count, me, lambda o: grad_copy(o, me).start())
    own_grad = pltpu.make_async_copy(grad_ref.at[me], dst_of(result_ref, me), own_sem.at[2])
    own_grad.start()
    each(count, me, lambda o: grad_copy(o, o).wait())
    own_grad.wait()


def per_device(lensing_maps, filter_taps, survey_mask, bin_pairs, target_corr, pair_weight):
    scales, tap_count = filter_taps.shape
    half = (tap_count - 1) // 2
    strip = lensing_maps[0]
    strip_rows, cols = strip.shape
    bins, sky = lax.axis_size("bin"), lax.axis_size("sky")
    count = bins * sky
    pairs, lags = pair_weight.shape[0], pair_weight.shape[2]
    row_count = strip_rows * sky
    groups = row_count // XB
    chunk = cols // count
    width = round_up(chunk + 2 * (2 * half + lags - 1), 128)
    halo = (width - chunk) // 2
    out_width = round_up(chunk, 128)
    tiles = width // 128 + 1
    size = bins * XB
    aligned = chunk % 128 == 0

    windows = jnp.pad(strip, ((0, 0), (halo, halo)))
    if not aligned:
        windows = jnp.stack([windows[:, d * chunk : d * chunk + width] for d in range(count)])
    mark_width = round_up(survey_mask.shape[1] + 1 + tiles, 128)
    marks = jnp.pad(
        survey_mask.astype(F32), ((0, 0), (1, mark_width - survey_mask.shape[1] - 1))
    )
    marks = jnp.broadcast_to(marks, (strip_rows, mark_width))
    tall = max(width, round_up(row_count + 2 * half + 1, 128))
    taps = jnp.stack([filter_taps, filter_taps[:, ::-1]])
    taps = jnp.pad(taps, ((0, 0), (0, 0), (0, tall - tap_count)))[:, :, None, :]
    fit = jnp.stack([pair_weight, target_corr]).reshape(2, pairs, scales * lags)
    fit = jnp.tile(jnp.pad(fit, ((0, 0), (0, 0), (0, XB - scales * lags))), (1, 1, bins))

    if aligned:
        src_of = lambda ref, d: ref.at[:, pl.ds(pl.multiple_of(d * chunk, 128), width)]
        dst_of = lambda ref, d: ref.at[:, pl.ds(pl.multiple_of(d * chunk, 128), chunk)]
        result_shape = (strip_rows, cols)
    else:
        src_of = lambda ref, d: ref.at[d]
        dst_of = lambda ref, d: ref.at[d]
        result_shape = (count, strip_rows, out_width)

    spec = pl.BlockSpec(memory_space=pltpu.VMEM)
    table_shape = (bins, size)
    dma = pltpu.SemaphoreType.DMA
    result, corr = pl.pallas_call(
        functools.partial(
            step_kernel, bins, sky, scales, lags, groups, chunk, halo, tiles, half,
            1.0 / (row_count * cols), src_of, dst_of,
        ),
        out_shape=(
            jax.ShapeDtypeStruct(result_shape, F32),
            jax.ShapeDtypeStruct((pairs, size), F32),
        ),
        in_specs=[spec] * 5,
        out_specs=(spec, spec),
        scratch_shapes=[
            pltpu.VMEM((count, strip_rows, width), BF16),
            pltpu.VMEM((sky, strip_rows, mark_width), F32),
            pltpu.VMEM((groups, scales, size, width), BF16),
            pltpu.VMEM((groups, scales, size, width), BF16),
            pltpu.VMEM((groups, scales, size, width), BF16),
            pltpu.VMEM((scales * lags,) + table_shape, F32),
            pltpu.VMEM((count, strip_rows, out_width), F32),
            pltpu.VMEM((2, scales, width, width), BF16),
            pltpu.VMEM((2, scales, width, out_width), BF16),
            pltpu.VMEM(table_shape, F32),
            pltpu.VMEM((sky,) + table_shape, F32),
            pltpu.VMEM(table_shape, F32),
            pltpu.VMEM((bins,) + table_shape, F32),
            dma((count,)), dma((count,)), dma((sky,)), dma((sky,)), dma((sky,)), dma((sky,)),
            dma((bins,)), dma((bins,)), dma((count,)), dma((count,)), dma((3,)),
        ],
        compiler_params=pltpu.CompilerParams(
            collective_id=1, has_side_effects=True, vmem_limit_bytes=VMEM_LIMIT
        ),
    )(windows, marks, taps, bin_pairs, fit)
    if not aligned:
        result = jnp.transpose(result[:, :, :chunk], (1, 0, 2)).reshape(strip_rows, cols)
    corr_table = corr[:, : scales * lags].reshape(pairs, scales, lags)
    return (corr_table, result[None])


def solution(mesh):
    placed = (P("bin", "sky", None), P(), P("sky", None), P(), P(), P())
    return jax.shard_map(
        per_device,
        mesh=mesh,
        in_specs=placed,
        out_specs=(P(), P("bin", "sky", None)),
        check_vma=False,
    )
```

time: 307 us -> 59.2 us (0.19)
  waiting for transfers between devices: 133 us -> 0 us
  other arithmetic: 79.3 us -> 0.02 us
  Pallas kernels: 0 us -> 49.5 us
  blocking collectives: 47.8 us -> 0 us
  starting transfers between devices: 14.4 us -> 0 us
  local copies, waits for them, and re-layouts: 22 us -> 8.28 us
  matrix products: 8.21 us -> 0 us
    ppermute x11 -> x0, waiting for transfers between devices: 133 us -> none  [the longest x7 116 us: shifted(): return lax.ppermute(value, axis, pairs)]
    pallas_call x0 -> x1, Pallas kernels: none -> 49.5 us  [per_device(): pl.pallas_call(functools.partial(step_kernel, bins, sky, scales, lags, gr...]
    psum x1 -> x0, blocking collectives: 47.8 us -> none  [per_device(): pair_table = lax.psum(tables, ('bin', 'sky'))]
    add x17 -> x0, other arithmetic: 29.2 us -> none  [the longest x7 16.7 us: reread(): return totals + partner_term(visitor, k)]
    reduce_sum x30 -> x0, other arithmetic: 17 us -> none  [the longest x29 11.9 us: lagged(): columns.append(jnp.sum(product, axis=(1, 2)))]
    mul x53 -> x0, other arithmetic: 15.8 us -> none  [the longest x24 14.7 us: adjoint_lags(): joint_mask[None] * widened[:, :, offset:]]
    convert_element_type x31 -> x1, other arithmetic: 15.3 us -> 0.01 us  [per_device(): survey_mask.astype(F32)]
    ppermute x11 -> x0, starting transfers between devices: 14.4 us -> none  [the longest x2 8.95 us: with_halo(): lax.ppermute(lax.slice_in_dim(block, block.shape[dim] - width, None, axis...]
  transfers between devices with their start and end apart: 11 -> 0, of which waited for: 10 -> 0; matrix products, arithmetic and copies ran while one was open for 2% -> 0% of each run, Pallas kernels for 0% -> 0%
where the time goes in v1:
time: 59.2 us; the launch traced here: 58.5 us
  Pallas kernels  49.5 us (84%)
  local copies, waits for them, and re-layouts  8.28 us (14%)
  between operations  0.69 us (1%)
    pallas_call x1, Pallas kernels, per_device(): pl.pallas_call(functools.partial(step_kernel, bins, sky, scales, lags, gr...  49.5 us
    unnamed x15, local copies, waits for them, and re-layouts  3.9 us

profile of v1, /device:TPU:9, one launch (start us, length us, event | category | flops | bytes accessed | tf_op | source)
XLA Modules:
  0.0 58.5 jit_solution(6960444619461542926)
XLA Ops:
  0.6 0.0 copy-start.5
  0.6 0.6 %copy-done.5 = s32[1,64]{1,0:T(1,128)S(1)} copy-done((s32[1,64]{1,0:T(1,128)S(1)}, s32[1,64]{1,0:T(1,128)}, u32[]{:S(2)}) %copy-start.5) | copy-done | bytes 280
  1.3 0.0 copy-start.1
  1.3 0.0 copy-start.2
  1.3 0.1 pad_bitcast_fusion
  1.4 0.6 %broadcast_in_dim.14.mark_ref = f32[8,128]{1,0:T(8,128)} broadcast(f32[128]{0:T(128)S(1)} %pad_bitcast_fusion), dimensions={1} | broadcast | bytes 4608 | tf_op jit(solution)/shard_map/broadcast_in_dim | solution.py:325
  2.0 0.0 copy-done.1
  2.0 0.1 rev.3
  2.0 0.0 copy-done.2
  2.1 0.7 %copy-done.3 = f32[36,5,4]{0,2,1:T(4,128)S(1)} copy-done((f32[36,5,4]{0,2,1:T(4,128)S(1)}, f32[36,5,4]{0,2,1:T(4,128)}, u32[]{:S(2)}) %copy-start.3) | copy-done | bytes 2904
  2.8 0.1 copy.19
  2.9 0.0 copy-start.4
  2.9 0.6 %copy.13.tap_ref = f32[2,5,1,384]{3,2,1,0:T(1,128)} copy(f32[2,5,1,384]{3,1,0,2:T(8,128)S(1)} %fusion) | data formatting | bytes 30720 | tf_op jit(solution)/shard_map/broadcast_in_dim | solution.py:328
  3.5 0.1 copy-done.4
  3.6 0.7 %copy.14.pair_ref = s32[36,2]{1,0:T(8,128)} copy(s32[36,2]{0,1:T(2,128)S(1)} %copy-done.4) | data formatting | bytes 576 | tf_op args[3]
  4.3 0.0 copy-done
  4.3 0.8 %pad.16.x_ref = bf16[8,8320]{1,0:T(8,128)(2,1)} pad(bf16[8,8192]{1,0:T(8,128)(2,1)S(1)} %bitcast.19, bf16[]{:T(256)} %constant.3.clone.1), padding=0_0x64_64 | pad | bytes 264194 | tf_op jit(solution)/shard_map/jit(_pad)/pad | solution.py:318
  5.1 0.2 tile.10
  5.2 0.6 %copy.15.fit_ref = f32[2,36,256]{2,1,0:T(8,128)} copy(f32[2,36,256]{2,0,1:T(2,128)S(1)} %tile.10) | data formatting | bytes 147456 | tf_op jit(solution)/shard_map/tile | solution.py:330
  5.9 49.5 %shard_map.77 = (f32[8,8192]{1,0:T(8,128)}, f32[36,256]{1,0:T(8,128)}) custom-call(bf16[8,8320]{1,0:T(8,128)(2,1)} %pad.16.x_ref, f32[8,128]{1,0:T(8,128)} %broadcast_in_dim.14.mark_ref, f32[2,5,1,384]{3,2,1,0:T(1,128)} %copy.13.tap_ref, s32[36,2]{1,0:T(8,128)} %copy.14.pair_ref, f32[2,36,256]{2,1,0:T(8,128)} %copy.15.fit_ref), custom_call_target="tpu_custom_call" | custom-call | tf_op jit(solution)/shard_map/pallas_call | solution.py:344
  55.4 0.7 %slice.3 = f32[36,20]{1,0:T(8,128)S(1)} slice(f32[36,256]{1,0:T(8,128)} %get-tuple-element.4), slice={[0:36], [0:20]} | slice | bytes 5760 | tf_op jit(solution)/shard_map/slice | solution.py:378
  56.1 0.1 copy.16
  56.2 0.6 %reshape.16 = f32[36,5,4]{0,2,1:T(4,128)} reshape(f32[36,20]{0,1:T(8,128)S(1)} %copy.16) | data formatting | bytes 5760 | tf_op jit(solution)/shard_map/reshape | solution.py:378
  56.8 1.7 %copy.21 = f32[1,8,8192]{2,1,0:T(8,128)} copy(f32[1,8,8192]{2,1,0:T(8,128)} %bitcast.18) | data formatting | bytes 524288
  (9 shorter events, 0.1 us)
Async XLA Ops:
  0.6 0.7 %copy-start.5 = (s32[1,64]{1,0:T(1,128)S(1)}, s32[1,64]{1,0:T(1,128)}, u32[]{:S(2)}) copy-start(s32[1,64]{1,0:T(1,128)} %param.8) | copy-start | bytes 772
  1.3 0.7 %copy-start.1 = (f32[5,17]{1,0:T(8,128)S(1)}, f32[5,17]{1,0:T(8,128)}, u32[]{:S(2)}) copy-start(f32[5,17]{1,0:T(8,128)} %param.7) | copy-start | bytes 1024
  1.3 0.8 %copy-start.2 = (f32[36,5,4]{0,2,1:T(4,128)S(1)}, f32[36,5,4]{0,2,1:T(4,128)}, u32[]{:S(2)}) copy-start(f32[36,5,4]{0,2,1:T(4,128)} %param.10) | copy-start | bytes 8644
  2.0 0.7 %copy-start.3 = (f32[36,5,4]{0,2,1:T(4,128)S(1)}, f32[36,5,4]{0,2,1:T(4,128)}, u32[]{:S(2)}) copy-start(f32[36,5,4]{0,2,1:T(4,128)} %param.11) | copy-start | bytes 8644
  2.8 1.5 %copy-start = (bf16[1,8,8192]{2,1,0:T(8,128)(2,1)S(1)}, bf16[1,8,8192]{2,1,0:T(8,128)(2,1)}, u32[]{:S(2)}) copy-start(bf16[1,8,8192]{2,1,0:T(8,128)(2,1)} %param.6) | copy-start | bytes 393220
  2.9 0.7 %copy-start.4 = (s32[36,2]{0,1:T(2,128)S(1)}, s32[36,2]{0,1:T(2,128)}, u32[]{:S(2)}) copy-start(s32[36,2]{0,1:T(2,128)} %param.9) | copy-start | bytes 868

commit v2 on v1

--- a/solution.py
+++ b/solution.py
@@ -70,11 +70,12 @@
     result_ref, corr_ref,
     y_ref, marks_ref, hi_ref, lo_ref, g_ref, sums_ref, grad_ref,
     col_ref, adj_ref, part_ref, sky_ref, bin_in_ref, bin_ref,
-    send_x, recv_x, send_m, recv_m, send_s, recv_s, send_b, recv_b, send_g, recv_g, own_sem,
+    send_x, recv_x, send_m, recv_m, send_s, recv_s, send_b, recv_b, send_g, recv_g, own_sem, coef_ref,
 ):
     count = bins * sky
     strip_rows, width = y_ref.shape[1], y_ref.shape[2]
-    out_width = grad_ref.shape[2]
+    pieces, part_width = grad_ref.shape[0], grad_ref.shape[3]
+    span = adj_ref.shape[2]
     size = bins * XB
     rows = groups * XB
     my_bin, my_sky = lax.axis_index("bin"), lax.axis_index("sky")
@@ -123,7 +124,7 @@
         for at, part in enumerate(halves(band(turned[:, :width], width, width, half, width))):
             col_ref[at, s] = part
         for at, part in enumerate(
-            halves(band(taps[:, :width], width, width, half + halo, out_width))
+            halves(band(taps[:, :span], span, span, half + halo, part_width))
         ):
             adj_ref[at, s] = part
         a, b = halves(band(taps[:, :narrow], rows, narrow, half, rows))
@@ -246,55 +247,69 @@
             value = value + pltpu.roll(value, step, 1)
         return value
 
-    for g in range(groups):
-
-        def backward(s, carry):
-            maps = g_ref[g, s].astype(F32)
-            total_grad = jnp.zeros((size, width), F32)
-            for shift in range(1 - lags, lags):
-                moved = maps if shift == 0 else pltpu.roll(maps, (width - shift) % width, 1)
-                moved = moved.astype(BF16)
-                if shift == 0:
-                    coef = coefficient(ahead + behind, s * lags)
-                elif shift > 0:
-                    coef = coefficient(ahead, s * lags + shift)
-                else:
-                    coef = coefficient(behind, s * lags - shift)
-                full = jnp.broadcast_to(coef[:, None, :], (bins, XB, size)).reshape(size, size)
-                hi, lo = halves(full * diag)
-                total_grad = total_grad + mm(hi, moved) + mm(lo, moved)
-            total_grad = jnp.where(masks[g], total_grad, 0.0)
-            hi, lo = halves(mm3(halves(total_grad), (adj_ref[0, s], adj_ref[1, s])))
-            hi_ref[g, s, :, :out_width] = hi
-            lo_ref[g, s, :, :out_width] = lo
-            return carry
-
-        lax.fori_loop(0, scales, backward, 0)
-
-    for b in range(bins):
-        spots = [(g, s) for s in range(scales) for g in range(groups)]
-        rows_of = slice(b * XB, (b + 1) * XB)
-        hi = jnp.concatenate([hi_ref[g, s, rows_of, :out_width] for g, s in spots], axis=0)
-        lo = jnp.concatenate([lo_ref[g, s, rows_of, :out_width] for g, s in spots], axis=0)
-        total_rows = mm3(back, (hi, lo))
-        for k in range(sky):
-            grad_ref[b * sky + k] = total_rows[k * strip_rows : (k + 1) * strip_rows]
-
-    def grad_copy(other, slot):
+    def grad_copy(piece, other, slot):
         return pltpu.make_async_remote_copy(
-            src_ref=grad_ref.at[other],
-            dst_ref=dst_of(result_ref, slot),
-            send_sem=send_g.at[other],
-            recv_sem=recv_g.at[slot],
+            src_ref=grad_ref.at[piece, other],
+            dst_ref=dst_of(result_ref, slot, piece),
+            send_sem=send_g.at[piece, other],
+            recv_sem=recv_g.at[piece, slot],
             device_id=(other // sky, lax.rem(other, sky)),
             device_id_type=MESH,
         )
 
-    each(count, me, lambda o: grad_copy(o, me).start())
-    own_grad = pltpu.make_async_copy(grad_ref.at[me], dst_of(result_ref, me), own_sem.at[2])
-    own_grad.start()
-    each(count, me, lambda o: grad_copy(o, o).wait())
-    own_grad.wait()
+    own_grads = []
+    for piece in range(pieces):
+        cut = slice(piece * part_width, piece * part_width + span)
+        for g in range(groups):
+
+            def backward(s, carry):
+                maps = g_ref[g, s, :, cut].astype(F32)
+                total_grad = jnp.zeros((size, span), F32)
+                for shift in range(1 - lags, lags):
+                    moved = maps if shift == 0 else pltpu.roll(maps, (span - shift) % span, 1)
+                    moved = moved.astype(BF16)
+                    at = s * (2 * lags - 1) + shift + lags - 1
+                    if piece == 0:
+                        if shift == 0:
+                            coef = coefficient(ahead + behind, s * lags)
+                        elif shift > 0:
+                            coef = coefficient(ahead, s * lags + shift)
+                        else:
+                            coef = coefficient(behind, s * lags - shift)
+                        if pieces > 1 or groups > 1:
+                            coef_ref[at] = coef
+                    else:
+                        coef = coef_ref[at]
+                    full = jnp.broadcast_to(coef[:, None, :], (bins, XB, size))
+                    hi, lo = halves(full.reshape(size, size) * diag)
+                    total_grad = total_grad + mm(hi, moved) + mm(lo, moved)
+                total_grad = jnp.where(masks[g][:, cut], total_grad, 0.0)
+                hi, lo = halves(mm3(halves(total_grad), (adj_ref[0, s], adj_ref[1, s])))
+                hi_ref[g, s, :, :part_width] = hi
+                lo_ref[g, s, :, :part_width] = lo
+                return carry
+
+            lax.fori_loop(0, scales, backward, 0)
+
+        for b in range(bins):
+            spots = [(g, s) for s in range(scales) for g in range(groups)]
+            rows_of = slice(b * XB, (b + 1) * XB)
+            hi = jnp.concatenate([hi_ref[g, s, rows_of, :part_width] for g, s in spots], axis=0)
+            lo = jnp.concatenate([lo_ref[g, s, rows_of, :part_width] for g, s in spots], axis=0)
+            total_rows = mm3(back, (hi, lo))
+            for k in range(sky):
+                at = b * sky + k
+                grad_ref[piece, at] = total_rows[k * strip_rows : (k + 1) * strip_rows]
+
+        each(count, me, lambda o: grad_copy(piece, o, me).start())
+        own_grad = pltpu.make_async_copy(
+            grad_ref.at[piece, me], dst_of(result_ref, me, piece), own_sem.at[2 + piece]
+        )
+        own_grad.start()
+        own_grads.append(own_grad)
+    for piece in range(pieces):
+        each(count, me, lambda o: grad_copy(piece, o, o).wait())
+        own_grads[piece].wait()
 
 
 def per_device(lensing_maps, filter_taps, survey_mask, bin_pairs, target_corr, pair_weight):
@@ -314,6 +329,9 @@
     tiles = width // 128 + 1
     size = bins * XB
     aligned = chunk % 128 == 0
+    pieces = out_width // 128
+    part_width = out_width // pieces
+    span = width - (pieces - 1) * part_width
 
     windows = jnp.pad(strip, ((0, 0), (halo, halo)))
     if not aligned:
@@ -331,11 +349,13 @@
 
     if aligned:
         src_of = lambda ref, d: ref.at[:, pl.ds(pl.multiple_of(d * chunk, 128), width)]
-        dst_of = lambda ref, d: ref.at[:, pl.ds(pl.multiple_of(d * chunk, 128), chunk)]
+        dst_of = lambda ref, d, p: ref.at[
+            :, pl.ds(pl.multiple_of(d * chunk + p * part_width, 128), part_width)
+        ]
         result_shape = (strip_rows, cols)
     else:
         src_of = lambda ref, d: ref.at[d]
-        dst_of = lambda ref, d: ref.at[d]
+        dst_of = lambda ref, d, p: ref.at[d]
         result_shape = (count, strip_rows, out_width)
 
     spec = pl.BlockSpec(memory_space=pltpu.VMEM)
@@ -359,15 +379,16 @@
             pltpu.VMEM((groups, scales, size, width), BF16),
             pltpu.VMEM((groups, scales, size, width), BF16),
             pltpu.VMEM((scales * lags,) + table_shape, F32),
-            pltpu.VMEM((count, strip_rows, out_width), F32),
+            pltpu.VMEM((pieces, count, strip_rows, part_width), F32),
             pltpu.VMEM((2, scales, width, width), BF16),
-            pltpu.VMEM((2, scales, width, out_width), BF16),
+            pltpu.VMEM((2, scales, span, part_width), BF16),
             pltpu.VMEM(table_shape, F32),
             pltpu.VMEM((sky,) + table_shape, F32),
             pltpu.VMEM(table_shape, F32),
             pltpu.VMEM((bins,) + table_shape, F32),
             dma((count,)), dma((count,)), dma((sky,)), dma((sky,)), dma((sky,)), dma((sky,)),
-            dma((bins,)), dma((bins,)), dma((count,)), dma((count,)), dma((3,)),
+            dma((bins,)), dma((bins,)), dma((pieces, count)), dma((pieces, count)), dma((2 + pieces,)),
+            pltpu.VMEM((scales * (2 * lags - 1),) + table_shape, F32),
         ],
         compiler_params=pltpu.CompilerParams(
             collective_id=1, has_side_effects=True, vmem_limit_bytes=VMEM_LIMIT

time: 59.2 us -> 59 us (level)
  the two profiles are of different devices: /device:TPU:9 before, /device:TPU:0 now
where the time goes in v2:
time: 59 us; the launch traced here: 58.7 us
  Pallas kernels  49.7 us (84%)
  local copies, waits for them, and re-layouts  8.28 us (14%)
  between operations  0.69 us (1%)
    pallas_call x1, Pallas kernels, per_device(): pl.pallas_call(functools.partial(step_kernel, bins, sky, scales, lags, gr...  49.7 us
    unnamed x15, local copies, waits for them, and re-layouts  3.9 us

profile of v2, /device:TPU:0, one launch (start us, length us, event | category | flops | bytes accessed | tf_op | source)
XLA Modules:
  0.0 58.7 jit_solution(15674162518779208448)
XLA Ops:
  0.6 0.0 copy-start.5
  0.6 0.6 %copy-done.5 = s32[1,64]{1,0:T(1,128)S(1)} copy-done((s32[1,64]{1,0:T(1,128)S(1)}, s32[1,64]{1,0:T(1,128)}, u32[]{:S(2)}) %copy-start.5) | copy-done | bytes 280
  1.3 0.0 copy-start.1
  1.3 0.0 copy-start.2
  1.3 0.1 pad_bitcast_fusion
  1.4 0.6 %broadcast_in_dim.14.mark_ref = f32[8,128]{1,0:T(8,128)} broadcast(f32[128]{0:T(128)S(1)} %pad_bitcast_fusion), dimensions={1} | broadcast | bytes 4608 | tf_op jit(solution)/shard_map/broadcast_in_dim | solution.py:343
  2.0 0.0 copy-done.1
  2.0 0.1 rev.3
  2.0 0.0 copy-done.2
  2.1 0.7 %copy-done.3 = f32[36,5,4]{0,2,1:T(4,128)S(1)} copy-done((f32[36,5,4]{0,2,1:T(4,128)S(1)}, f32[36,5,4]{0,2,1:T(4,128)}, u32[]{:S(2)}) %copy-start.3) | copy-done | bytes 2904
  2.8 0.1 copy.19
  2.9 0.0 copy-start.4
  2.9 0.6 %copy.13.tap_ref = f32[2,5,1,384]{3,2,1,0:T(1,128)} copy(f32[2,5,1,384]{3,1,0,2:T(8,128)S(1)} %fusion) | data formatting | bytes 30720 | tf_op jit(solution)/shard_map/broadcast_in_dim | solution.py:346
  3.5 0.1 copy-done.4
  3.6 0.7 %copy.14.pair_ref = s32[36,2]{1,0:T(8,128)} copy(s32[36,2]{0,1:T(2,128)S(1)} %copy-done.4) | data formatting | bytes 576 | tf_op args[3]
  4.3 0.0 copy-done
  4.3 0.8 %pad.16.x_ref = bf16[8,8320]{1,0:T(8,128)(2,1)} pad(bf16[8,8192]{1,0:T(8,128)(2,1)S(1)} %bitcast.19, bf16[]{:T(256)} %constant.3.clone.1), padding=0_0x64_64 | pad | bytes 264194 | tf_op jit(solution)/shard_map/jit(_pad)/pad | solution.py:336
  5.1 0.2 tile.10
  5.2 0.6 %copy.15.fit_ref = f32[2,36,256]{2,1,0:T(8,128)} copy(f32[2,36,256]{2,0,1:T(2,128)S(1)} %tile.10) | data formatting | bytes 147456 | tf_op jit(solution)/shard_map/tile | solution.py:348
  5.9 49.7 %shard_map.77 = (f32[8,8192]{1,0:T(8,128)}, f32[36,256]{1,0:T(8,128)}) custom-call(bf16[8,8320]{1,0:T(8,128)(2,1)} %pad.16.x_ref, f32[8,128]{1,0:T(8,128)} %broadcast_in_dim.14.mark_ref, f32[2,5,1,384]{3,2,1,0:T(1,128)} %copy.13.tap_ref, s32[36,2]{1,0:T(8,128)} %copy.14.pair_ref, f32[2,36,256]{2,1,0:T(8,128)} %copy.15.fit_ref), custom_call_target="tpu_custom_call" | custom-call | tf_op jit(solution)/shard_map/pallas_call | solution.py:364
  55.6 0.7 %slice.3 = f32[36,20]{1,0:T(8,128)S(1)} slice(f32[36,256]{1,0:T(8,128)} %get-tuple-element.4), slice={[0:36], [0:20]} | slice | bytes 5760 | tf_op jit(solution)/shard_map/slice | solution.py:399
  56.3 0.1 copy.16
  56.4 0.6 %reshape.16 = f32[36,5,4]{0,2,1:T(4,128)} reshape(f32[36,20]{0,1:T(8,128)S(1)} %copy.16) | data formatting | bytes 5760 | tf_op jit(solution)/shard_map/reshape | solution.py:399
  57.0 1.7 %copy.21 = f32[1,8,8192]{2,1,0:T(8,128)} copy(f32[1,8,8192]{2,1,0:T(8,128)} %bitcast.18) | data formatting | bytes 524288
  (9 shorter events, 0.1 us)
Async XLA Ops:
  0.6 0.7 %copy-start.5 = (s32[1,64]{1,0:T(1,128)S(1)}, s32[1,64]{1,0:T(1,128)}, u32[]{:S(2)}) copy-start(s32[1,64]{1,0:T(1,128)} %param.8) | copy-start | bytes 772
  1.3 0.7 %copy-start.1 = (f32[5,17]{1,0:T(8,128)S(1)}, f32[5,17]{1,0:T(8,128)}, u32[]{:S(2)}) copy-start(f32[5,17]{1,0:T(8,128)} %param.7) | copy-start | bytes 1024
  1.3 0.8 %copy-start.2 = (f32[36,5,4]{0,2,1:T(4,128)S(1)}, f32[36,5,4]{0,2,1:T(4,128)}, u32[]{:S(2)}) copy-start(f32[36,5,4]{0,2,1:T(4,128)} %param.10) | copy-start | bytes 8644
  2.0 0.7 %copy-start.3 = (f32[36,5,4]{0,2,1:T(4,128)S(1)}, f32[36,5,4]{0,2,1:T(4,128)}, u32[]{:S(2)}) copy-start(f32[36,5,4]{0,2,1:T(4,128)} %param.11) | copy-start | bytes 8644
  2.8 1.5 %copy-start = (bf16[1,8,8192]{2,1,0:T(8,128)(2,1)S(1)}, bf16[1,8,8192]{2,1,0:T(8,128)(2,1)}, u32[]{:S(2)}) copy-start(bf16[1,8,8192]{2,1,0:T(8,128)(2,1)} %param.6) | copy-start | bytes 393220
  2.9 0.7 %copy-start.4 = (s32[36,2]{0,1:T(2,128)S(1)}, s32[36,2]{0,1:T(2,128)}, u32[]{:S(2)}) copy-start(s32[36,2]{0,1:T(2,128)} %param.9) | copy-start | bytes 868
